TPU v7x, 128 devices: a whole 4x4x4 slice. The times are simulated.
128 devices in a mesh: ctx: 64 (over y, x, z), head: 2 (over core).
Axes of the slice: x: 4, y: 4, z: 4, core: 2. Of those that a mesh axis runs over, the one named last changes fastest.
Arguments:
- queries: float32 [16384, 2048], P('ctx', 'head')
- keys: float32 [16384, 512], P(('ctx', 'head'))
- values: float32 [16384, 512], P(('ctx', 'head')), may hold values from -6 to 6
- cotangent: float32 [16384, 2048], P('ctx', 'head'), may hold values from -6 to 6
- selected: int32 [16, 3], replicated, may hold values from -1 to 15, as said below
Outputs:
- attended: float32 [16384, 2048], P('ctx', 'head')
- grad_queries: float32 [16384, 2048], P('ctx', 'head')
- grad_keys: float32 [16384, 512], P(('ctx', 'head'))
- grad_values: float32 [16384, 512], P(('ctx', 'head'))
Inputs may be any that keep to these rules, and one draw needn't show every extreme that they name: selected[b, 0] = b; entries 1 and 2 of row b are different blocks before b, except that an entry is -1 when no further block before b is left: row 0 is [0, -1, -1] and row 1 is [1, 0, -1].
All inputs are finite; a program needn't handle non-finite values.
Results may differ from a plain program's by a relative error of at most 0.0003.
Values sent between devices are 32-bit elements; how exact they have to be, the bound alone decides.
No kernel may reach another device: no remote copies, remote signals or barrier semaphores. Data moves between devices by JAX's collectives and lax.ppermute only.
A program may use at most 192 MiB of HBM per device.

v0:
```python
import math
import jax
import jax.numpy as jnp
from jax import lax
from jax.sharding import PartitionSpec as P

QUERY_HEADS = 16
KEY_VALUE_HEADS = 4
HEAD_WIDTH = 128
BLOCK_TOKENS = 1024
TOPK = 3


def block_masks(selected, block_index, query_pos):
    masks = []
    for slot_index in range(TOPK):
        chosen = selected[block_index, slot_index]
        if slot_index == 0:
            key_pos = block_index * BLOCK_TOKENS + jnp.arange(BLOCK_TOKENS, dtype=jnp.int32)
            masks.append(key_pos[None, :] <= query_pos[:, None])
        else:
            masks.append(jnp.broadcast_to(chosen >= 0, (query_pos.shape[0], BLOCK_TOKENS)))
    return jnp.concatenate(masks, 1)


def pick_blocks(whole_keys, whole_values, selected, block_index, kv_heads):
    key_parts, value_parts, offsets = ([], [], [])
    for slot_index in range(TOPK):
        chosen = selected[block_index, slot_index]
        offset = jnp.maximum(chosen, 0) * BLOCK_TOKENS
        offsets.append(offset)
        key_parts.append(lax.dynamic_slice_in_dim(whole_keys, offset, BLOCK_TOKENS, 0))
        value_parts.append(lax.dynamic_slice_in_dim(whole_values, offset, BLOCK_TOKENS, 0))
    picked_keys = jnp.concatenate(key_parts, 0).reshape(TOPK * BLOCK_TOKENS, kv_heads, HEAD_WIDTH)
    picked_values = jnp.concatenate(value_parts, 0).reshape(
        TOPK * BLOCK_TOKENS, kv_heads, HEAD_WIDTH
    )
    return (picked_keys, picked_values, offsets)


def shards(queries, keys, values, cotangent, selected):
    highest = lax.Precision.HIGHEST
    scaling = 1.0 / math.sqrt(HEAD_WIDTH)
    group_width = QUERY_HEADS // KEY_VALUE_HEADS
    local_keys, local_values = (
        lax.all_to_all(keys, "head", split_axis=1, concat_axis=0, tiled=True),
        lax.all_to_all(values, "head", split_axis=1, concat_axis=0, tiled=True),
    )
    tokens_here = local_keys.shape[0]
    width = local_keys.shape[1]
    kv_heads = width // HEAD_WIDTH
    first_position = lax.axis_index("ctx") * tokens_here
    block_index = first_position // BLOCK_TOKENS
    query_pos = first_position + jnp.arange(tokens_here, dtype=jnp.int32)
    allowed = block_masks(selected, block_index, query_pos)
    whole_keys, whole_values = (
        lax.all_gather(local_keys, "ctx", axis=0, tiled=True),
        lax.all_gather(local_values, "ctx", axis=0, tiled=True),
    )
    picked_keys, picked_values, offsets = pick_blocks(
        whole_keys, whole_values, selected, block_index, kv_heads
    )
    block_of_queries = queries.reshape(tokens_here, kv_heads, group_width, HEAD_WIDTH)
    cotangent_block = cotangent.reshape(tokens_here, kv_heads, group_width, HEAD_WIDTH)
    scores = scaling * jnp.einsum(
        "thgd,shd->hgts", block_of_queries, picked_keys, precision=highest
    )
    scores = jnp.where(allowed[None, None], scores, -jnp.inf)
    maximum = jnp.max(scores, axis=-1, keepdims=True)
    probs = jnp.exp(scores - maximum)
    probs = probs / jnp.sum(probs, axis=-1, keepdims=True)
    attended = jnp.einsum("hgts,shd->thgd", probs, picked_values, precision=highest)
    row_dots = jnp.transpose(jnp.sum(cotangent_block * attended, axis=-1), (1, 2, 0))
    grad_probs = jnp.einsum("thgd,shd->hgts", cotangent_block, picked_values, precision=highest)
    grad_scores = probs * (grad_probs - row_dots[..., None])
    query_gradient = scaling * jnp.einsum(
        "hgts,shd->thgd", grad_scores, picked_keys, precision=highest
    )
    grad_k_sel = scaling * jnp.einsum(
        "hgts,thgd->shd", grad_scores, block_of_queries, precision=highest
    )
    grad_v_sel = jnp.einsum("hgts,thgd->shd", probs, cotangent_block, precision=highest)
    seq_rows = whole_keys.shape[0]
    key_gradient_total = jnp.zeros((seq_rows, kv_heads, HEAD_WIDTH), jnp.float32)
    value_gradient_total = jnp.zeros((seq_rows, kv_heads, HEAD_WIDTH), jnp.float32)
    for slot_index in range(TOPK):
        offset = offsets[slot_index]
        piece_k = grad_k_sel[slot_index * BLOCK_TOKENS : (slot_index + 1) * BLOCK_TOKENS]
        piece_v = grad_v_sel[slot_index * BLOCK_TOKENS : (slot_index + 1) * BLOCK_TOKENS]
        key_gradient_total = lax.dynamic_update_slice_in_dim(
            key_gradient_total,
            lax.dynamic_slice_in_dim(key_gradient_total, offset, BLOCK_TOKENS, 0) + piece_k,
            offset,
            0,
        )
        value_gradient_total = lax.dynamic_update_slice_in_dim(
            value_gradient_total,
            lax.dynamic_slice_in_dim(value_gradient_total, offset, BLOCK_TOKENS, 0) + piece_v,
            offset,
            0,
        )
    owned_k, owned_v = (
        lax.psum_scatter(
            key_gradient_total.reshape(seq_rows, width), "ctx", scatter_dimension=0, tiled=True
        ),
        lax.psum_scatter(
            value_gradient_total.reshape(seq_rows, width), "ctx", scatter_dimension=0, tiled=True
        ),
    )
    grad_keys, grad_values = (
        lax.all_to_all(owned_k, "head", split_axis=0, concat_axis=1, tiled=True),
        lax.all_to_all(owned_v, "head", split_axis=0, concat_axis=1, tiled=True),
    )
    return (
        attended.reshape(tokens_here, -1),
        query_gradient.reshape(tokens_here, -1),
        grad_keys,
        grad_values,
    )


def solution(mesh):
    placed = (
        P("ctx", "head"),
        P(("ctx", "head"), None),
        P(("ctx", "head"), None),
        P("ctx", "head"),
        P(),
    )
    return jax.shard_map(
        shards,
        mesh=mesh,
        in_specs=placed,
        out_specs=(
            P("ctx", "head"),
            P("ctx", "head"),
            P(("ctx", "head"), None),
            P(("ctx", "head"), None),
        ),
        check_vma=False,
    )
```

profile of v0, /device:TPU:1, one launch (start us, length us, event | category | flops | bytes accessed | tf_op | source)
XLA Modules:
  0.0 1183.8 jit_solution(17859586762684518673)
XLA Ops:
  8.3 5.0 all_to_all.76
  15.4 3.9 all_to_all.77
  20.3 1.4 constant_dynamic-slice_fusion.6
  24.8 2.5 copy.85
  27.3 2.6 copy.115
  30.1 3.9 add_add_fusion
  34.1 86.8 %all-gather.5.cloned.1.call-done = f32[16384,256]{1,0:T(8,128)} async-done(((f32[256,256]{1,0:T(8,128)}), f32[16384,256]{1,0:T(8,128)}) %all-gather.5.cloned.1.call-update) | async-done | bytes 16777232 | tf_op jit(solution)/shard_map/all_gather | solution.py:57
  120.9 2.2 constant_dynamic-slice_fusion.2
  123.1 1.8 pad_maximum_fusion.1
  124.9 2.4 copy.81
  127.3 24.6 %fusion.3 = (f32[2,4,256]{2,1,0:T(4,128)S(1)}, f32[2,3072,256,4]{2,1,3,0:T(8,128)S(1)}) fusion(pred[256,3072]{0,1:T(8,128)(4,1)} %add_add_fusion, f32[3072,2,128,1]{0,2,3,1:T(8,128)S(1)} %bitcast.93, f32[256,2,4,128]{0,3,2,1:T(8,128)} %bitcast.95), kind=kOutput, calls=%fused_computation.6 | convolution fusion | flops 9682548736 | bytes 30154752 | tf_op jit(solution)/shard_map/thgd,shd->hgts/dot_general | solution.py:65
  151.9 8.6 copy-done
  160.6 5.3 fusion.2
  165.8 77.2 %all-gather.3.cloned.1.call-done = f32[16384,256]{0,1:T(8,128)} async-done(((f32[256,256]{0,1:T(8,128)}), f32[16384,256]{0,1:T(8,128)}) %all-gather.3.cloned.1.call-update) | async-done | bytes 16777232 | tf_op jit(solution)/shard_map/all_gather | solution.py:58
  243.1 2.3 constant_dynamic-slice_fusion.5
  245.3 2.0 pad_maximum_fusion
  247.3 25.6 %fusion.10 = (f32[256,2,4]{0,2,1:T(4,128)S(1)}, f32[2,128,4,256]{3,1,2,0:T(8,128)}) fusion(f32[256,1024]{0,1:T(8,128)S(1)} %copy-done.7, f32[3072,2,128,1]{0,2,3,1:T(8,128)} %bitcast.98, f32[2,3072,256,4]{2,1,3,0:T(8,128)} %copy-done, f32[2,4,256]{2,1,0:T(4,128)S(1)} %fusion.2, f32[2,4,256]{2,1,0:T(4,128)S(1)} %get-tuple-element.33, ...), kind=kOutput, calls=%fused_computation.26 | convolution fusion | flops 9689364480 | bytes 31219712 | tf_op jit(solution)/shard_map/hgts,shd->thgd/dot_general | solution.py:72
  272.9 34.7 %convolution_bitcast_fusion = f32[3072,2,128]{0,2,1:T(8,128)S(1)} fusion(f32[256,2,4,128]{0,3,2,1:T(8,128)S(1)} %bitcast.100, f32[2,3072,256,4]{2,1,3,0:T(8,128)} %copy-done, f32[2,4,256]{2,1,0:T(4,128)S(1)} %fusion.2, f32[2,4,256]{2,1,0:T(4,128)S(1)} %get-tuple-element.33, pred[256,3072]{0,1:T(8,128)(4,1)S(1)} %copy-done.5), kind=kOutput, calls=%fused_computation.7 | convolution fusion | flops 9688842240 | bytes 30162944 | tf_op jit(solution)/shard_map/hgts,thgd->shd/dot_general | solution.py:82
  307.7 34.6 %fusion = f32[2,4,256,3072]{2,3,1,0:T(8,128)} fusion(f32[2,4,256]{2,1,0:T(4,128)S(1)} %bitcast.112, f32[3072,2,128,1]{0,2,3,1:T(8,128)} %bitcast.99, f32[256,2,4,128]{0,3,2,1:T(8,128)S(1)} %bitcast.101, f32[2,4,256]{2,1,0:T(4,128)S(1)} %fusion.2, f32[2,4,256]{2,1,0:T(4,128)S(1)} %get-tuple-element.33, f32[2,3072,256,4]{2,1,3,0:T(8,128)} %copy-done, ...), kind=kOutput, calls=%fused_computation.1 | convolution fusion | flops 9701425152 | bytes 55336960 | tf_op jit(solution)/shard_map/thgd,shd->hgts/dot_general | solution.py:74
  342.2 29.3 %fusion.5 = f32[3072,2,128]{0,2,1:T(8,128)S(1)} fusion(f32[2,4,256,3072]{2,3,1,0:T(8,128)} %fusion, f32[256,2,4,128]{0,3,2,1:T(8,128)S(1)} %bitcast.96), kind=kOutput, calls=%fused_computation.10 | convolution fusion | flops 9664462848 | bytes 29360128 | tf_op jit(solution)/shard_map/hgts,thgd->shd/dot_general | solution.py:79
  371.5 7.7 broadcast.22.clone
  380.2 7.7 broadcast.22.clone.1
  389.0 3.4 fusion.7
  392.4 2.3 fusion.8
  394.8 2.8 fusion.6
  397.7 2.5 copy.96
  400.2 18.0 %convolution_multiply_fusion = f32[2,128,4,256]{3,1,2,0:T(8,128)} fusion(f32[3072,2,128,1]{0,2,3,1:T(8,128)S(1)} %bitcast.94, f32[2,4,256,3072]{2,3,1,0:T(8,128)} %fusion), kind=kOutput, calls=%fused_computation.14 | convolution fusion | flops 9663938560 | bytes 29360128 | tf_op jit(solution)/shard_map/hgts,shd->thgd/dot_general | solution.py:76
  418.2 2.5 copy.97
  420.7 313.6 %reduce-scatter.3.cloned.1.call-done = f32[256,256]{0,1:T(8,128)} async-done(((f32[16384,256]{0,1:T(8,128)}), f32[256,256]{0,1:T(8,128)}) %reduce-scatter.3.cloned.1.call-update) | async-done | bytes 262160 | tf_op jit(solution)/shard_map/reduce_scatter | solution.py:103
  735.4 54.5 %all_to_all.78 = f32[2,128,256]{2,1,0:T(8,128)S(1)} all-to-all(f32[2,128,256]{2,1,0:T(8,128)S(1)} %bitcast.106), channel_id=1, replica_groups=mesh['ctx'=64,'head'=2] {'head'}, dimensions={0} | all-to-all | bytes 524288 | tf_op jit(solution)/shard_map/all_to_all | solution.py:111
  790.9 329.5 %reduce-scatter.5.cloned.1.call-done = f32[256,256]{0,1:T(8,128)} async-done(((f32[16384,256]{0,1:T(8,128)}), f32[256,256]{0,1:T(8,128)}) %reduce-scatter.5.cloned.1.call-update) | async-done | bytes 262160 | tf_op jit(solution)/shard_map/reduce_scatter | solution.py:106
  1121.5 54.6 %all_to_all.79 = f32[2,128,256]{2,1,0:T(8,128)S(1)} all-to-all(f32[2,128,256]{2,1,0:T(8,128)S(1)} %bitcast.108), channel_id=1, replica_groups=mesh['ctx'=64,'head'=2] {'head'}, dimensions={0} | all-to-all | bytes 524288 | tf_op jit(solution)/shard_map/all_to_all | solution.py:112
  (43 shorter events, 10.7 us)
Async XLA Ops:
  7.2 113.7 %all-gather.5.cloned.1.call-start = ((), (), s32[]{:S(2)}) async-start(), calls=%async_computation.7 | async-start | bytes 17039360 | tf_op jit(solution)/shard_map/all_gather | solution.py:57
  14.2 228.9 %all-gather.3.cloned.1.call-start = ((), (), s32[]{:S(2)}) async-start(), calls=%async_computation.6 | async-start | bytes 17039360 | tf_op jit(solution)/shard_map/all_gather | solution.py:58
  20.2 714.1 %reduce-scatter.3.cloned.1.call-start = ((), (), s32[]{:S(2)}) async-start(), calls=%async_computation.8 | async-start | bytes 17039360 | tf_op jit(solution)/shard_map/reduce_scatter | solution.py:103
  127.3 24.6 %copy-start.1 = (f32[3072,256]{0,1:T(8,128)}, f32[3072,256]{0,1:T(8,128)S(1)}, u32[]{:S(2)}) copy-start(f32[3072,256]{0,1:T(8,128)S(1)} %copy.81) | copy-start | bytes 9437188
  127.3 33.3 %copy-start.4 = (pred[256,3072]{0,1:T(8,128)(4,1)S(1)}, pred[256,3072]{0,1:T(8,128)(4,1)}, u32[]{:S(2)}) copy-start(pred[256,3072]{0,1:T(8,128)(4,1)} %add_add_fusion) | copy-start | bytes 2359300
  151.9 8.7 copy-start
  160.6 86.7 %copy-start.5 = (pred[256,3072]{0,1:T(8,128)(4,1)S(1)}, pred[256,3072]{0,1:T(8,128)(4,1)}, u32[]{:S(2)}) copy-start(pred[256,3072]{0,1:T(8,128)(4,1)} %add_add_fusion) | copy-start | bytes 2359300
  160.6 86.7 %copy-start.7 = (f32[256,1024]{0,1:T(8,128)S(1)}, f32[256,1024]{0,1:T(8,128)}, u32[]{:S(2)}) copy-start(f32[256,1024]{0,1:T(8,128)} %copy.85) | copy-start | bytes 3145732
  307.6 81.3 %copy-start.6 = (f32[3072,2,128]{0,2,1:T(8,128)}, f32[3072,2,128]{0,2,1:T(8,128)S(1)}, u32[]{:S(2)}) copy-start(f32[3072,2,128]{0,2,1:T(8,128)S(1)} %convolution_bitcast_fusion) | copy-start | bytes 9437188
  307.7 34.6 %copy-start.3 = (f32[256,1024]{0,1:T(8,128)S(1)}, f32[256,1024]{0,1:T(8,128)}, u32[]{:S(2)}) copy-start(f32[256,1024]{0,1:T(8,128)} %copy.115) | copy-start | bytes 3145732
  394.7 5.5 copy-start.2
  394.7 725.6 %reduce-scatter.5.cloned.1.call-start = ((), (), s32[]{:S(2)}) async-start(), calls=%async_computation.9 | async-start | bytes 17039360 | tf_op jit(solution)/shard_map/reduce_scatter | solution.py:106
Sparse Core Ops, SparseCore 0:
  14.3 106.5 all-gather.4
  124.1 118.8 all-gather.2
  394.9 339.4 reduce-scatter.2
  736.6 383.7 reduce-scatter.4
where the time goes:
time: 1190 us; the launch traced here: 1180 us
  waiting for transfers between devices  807 us (68%)
  matrix products  167 us (14%)
  blocking collectives  118 us (10%)
  local copies, waits for them, and re-layouts  52.6 us (4%)
  other arithmetic  21.8 us (2%)
  between operations  17.2 us (1%)
    reduce_scatter x1, waiting for transfers between devices, shards(): lax.psum_scatter(value_gradient_total.reshape(seq_rows, width), 'ctx', sc...  330 us
    reduce_scatter x1, waiting for transfers between devices, shards(): lax.psum_scatter(key_gradient_total.reshape(seq_rows, width), 'ctx', scat...  314 us
    all_gather x1, waiting for transfers between devices, shards(): lax.all_gather(local_keys, 'ctx', axis=0, tiled=True)  86.8 us
    all_gather x1, waiting for transfers between devices, shards(): lax.all_gather(local_values, 'ctx', axis=0, tiled=True)  77.2 us
    all_to_all x1, blocking collectives, shards(): lax.all_to_all(owned_v, 'head', split_axis=0, concat_axis=1, tiled=True)  54.6 us
    all_to_all x1, blocking collectives, shards(): lax.all_to_all(owned_k, 'head', split_axis=0, concat_axis=1, tiled=True)  54.5 us
    dot_general x1, matrix products, shards(): jnp.einsum('hgts,thgd->shd', probs, cotangent_block, precision=highest)  34.7 us
    dot_general x1, matrix products, shards(): jnp.einsum('thgd,shd->hgts', cotangent_block, picked_values, precision=hi...  34.6 us
  transfers between devices with their start and end apart: 4, of which 4 were waited for; matrix products, arithmetic and copies ran while one was open for 6% of the time, Pallas kernels for 0%

commit v1 on v0

--- a/solution.py
+++ b/solution.py
@@ -1,3 +1,4 @@
+import functools
 import math
 import jax
 import jax.numpy as jnp
@@ -9,6 +10,21 @@
 HEAD_WIDTH = 128
 BLOCK_TOKENS = 1024
 TOPK = 3
+
+
+def resolve_patches(state, chip_axis):
+    return jnp.concatenate(
+        lax.all_to_all(
+            jnp.stack(lax.axis_size(chip_axis) * [state], 0),
+            concat_axis=0,
+            split_axis=0,
+            axis_name=chip_axis,
+        ),
+        0,
+    )
+
+
+bring_spot = functools.partial(resolve_patches, chip_axis="ctx")
 
 
 def block_masks(selected, block_index, query_pos):
@@ -54,7 +70,7 @@
     query_pos = first_position + jnp.arange(tokens_here, dtype=jnp.int32)
     allowed = block_masks(selected, block_index, query_pos)
     whole_keys, whole_values = (
-        lax.all_gather(local_keys, "ctx", axis=0, tiled=True),
+        bring_spot(local_keys),
         lax.all_gather(local_values, "ctx", axis=0, tiled=True),
     )
     picked_keys, picked_values, offsets = pick_blocks(

time: 1190 us -> 1260 us (1.059)
  waiting for transfers between devices: 807 us -> 861 us
  local copies, waits for them, and re-layouts: 52.6 us -> 65.3 us
    all_to_all x0 -> x1, waiting for transfers between devices: none -> 281 us  [resolve_patches(): lax.all_to_all(jnp.stack(lax.axis_size(chip_axis) * [state], 0), concat_a...]
    reduce_scatter x1, waiting for transfers between devices: 330 us -> 226 us  [shards(): lax.psum_scatter(value_gradient_total.reshape(seq_rows, width), 'ctx', sc...]
    all_gather x1 -> x0, waiting for transfers between devices: 86.8 us -> none  [shards(): lax.all_gather(local_keys, 'ctx', axis=0, tiled=True)]
    all_gather x1, waiting for transfers between devices: 77.2 us -> 21.9 us  [shards(): lax.all_gather(local_values, 'ctx', axis=0, tiled=True)]
    reduce_scatter x1, waiting for transfers between devices: 314 us -> 333 us  [shards(): lax.psum_scatter(key_gradient_total.reshape(seq_rows, width), 'ctx', scat...]
  transfers between devices with their start and end apart: 4 -> 4, of which waited for: 4 -> 4; matrix products, arithmetic and copies ran while one was open for 6% -> 13% of each run, Pallas kernels for 0% -> 0%
where the time goes in v1:
time: 1260 us; the launch traced here: 1250 us
  waiting for transfers between devices  861 us (68%)
  matrix products  164 us (13%)
  blocking collectives  112 us (9%)
  local copies, waits for them, and re-layouts  65.3 us (5%)
  other arithmetic  22.8 us (2%)
  between operations  17.7 us (1%)
    reduce_scatter x1, waiting for transfers between devices, shards(): lax.psum_scatter(key_gradient_total.reshape(seq_rows, width), 'ctx', scat...  333 us
    all_to_all x1, waiting for transfers between devices, resolve_patches(): lax.all_to_all(jnp.stack(lax.axis_size(chip_axis) * [state], 0), concat_a...  281 us
    reduce_scatter x1, waiting for transfers between devices, shards(): lax.psum_scatter(value_gradient_total.reshape(seq_rows, width), 'ctx', sc...  226 us
    all_to_all x1, blocking collectives, shards(): lax.all_to_all(owned_k, 'head', split_axis=0, concat_axis=1, tiled=True)  52.9 us
    all_to_all x1, blocking collectives, shards(): lax.all_to_all(owned_v, 'head', split_axis=0, concat_axis=1, tiled=True)  50.3 us
    dot_general x1, matrix products, shards(): jnp.einsum('hgts,thgd->shd', probs, cotangent_block, precision=highest)  34.9 us
    dot_general x1, matrix products, shards(): jnp.einsum('thgd,shd->hgts', cotangent_block, picked_values, precision=hi...  33.5 us
    dot_general x1, matrix products, shards(): jnp.einsum('hgts,thgd->shd', grad_scores, block_of_queries, precision=hig...  29.4 us
  transfers between devices with their start and end apart: 4, of which 4 were waited for; matrix products, arithmetic and copies ran while one was open for 13% of the time, Pallas kernels for 0%

profile of v1, /device:TPU:1, one launch (start us, length us, event | category | flops | bytes accessed | tf_op | source)
XLA Modules:
  0.0 1254.5 jit_solution(1029927319020621291)
XLA Ops:
  8.4 5.0 all_to_all.78
  15.4 3.9 all_to_all.79
  19.6 7.8 stack.5
  27.4 11.7 all-to-all-start.2
  43.4 1.3 copy.87
  44.9 3.9 add_add_fusion
  48.9 280.5 %all-to-all-done.2 = f32[64,256,256]{1,2,0:T(8,128)} async-done(((f32[64,256,256]{1,2,0:T(8,128)}), f32[64,256,256]{1,2,0:T(8,128)}, u32[]{:S(2)}, u32[]{:S(2)}) %all-to-all-start.2) | async-done | bytes 16777248 | tf_op jit(solution)/shard_map/all_to_all | solution.py:17
  329.4 11.7 copy.118
  341.1 21.9 %all-gather.2.cloned.1.call-done = f32[16384,256]{0,1:T(8,128)} async-done(((f32[256,256]{0,1:T(8,128)}), f32[16384,256]{0,1:T(8,128)}) %all-gather.2.cloned.1.call-update) | async-done | bytes 16777232 | tf_op jit(solution)/shard_map/all_gather | solution.py:74
  362.9 4.8 constant_dynamic-slice_fusion.2
  368.1 22.8 %fusion.3 = (f32[2,4,256]{2,1,0:T(4,128)S(1)}, f32[2,3072,256,4]{2,1,3,0:T(8,128)S(1)}) fusion(pred[256,3072]{0,1:T(8,128)(4,1)S(1)} %copy-done.3, f32[3072,2,128,1]{0,2,3,1:T(8,128)S(1)} %bitcast.96, f32[256,2,4,128]{0,3,2,1:T(8,128)S(1)} %bitcast.98), kind=kOutput, calls=%fused_computation.6 | convolution fusion | flops 9682548736 | bytes 30154752 | tf_op jit(solution)/shard_map/thgd,shd->hgts/dot_general | solution.py:81
  390.9 8.7 copy-done
  399.6 5.4 fusion.2
  405.0 34.9 %convolution_bitcast_fusion = f32[3072,2,128]{0,2,1:T(8,128)S(1)} fusion(f32[256,2,4,128]{0,3,2,1:T(8,128)S(1)} %bitcast.103, f32[2,3072,256,4]{2,1,3,0:T(8,128)} %copy-done, f32[2,4,256]{2,1,0:T(4,128)S(1)} %fusion.2, f32[2,4,256]{2,1,0:T(4,128)S(1)} %get-tuple-element.33, pred[256,3072]{0,1:T(8,128)(4,1)S(1)} %copy-done.3), kind=kOutput, calls=%fused_computation.7 | convolution fusion | flops 9688842240 | bytes 30162944 | tf_op jit(solution)/shard_map/hgts,thgd->shd/dot_general | solution.py:98
  440.0 7.7 broadcast.23.clone.1
  448.7 2.4 fusion.7
  451.1 2.4 fusion.6
  453.5 3.2 pad_maximum_fusion
  456.7 25.3 %fusion.10 = (f32[256,2,4]{0,2,1:T(4,128)S(1)}, f32[2,128,4,256]{3,1,2,0:T(8,128)}) fusion(f32[256,1024]{0,1:T(8,128)} %copy.87, f32[3072,2,128,1]{0,2,3,1:T(8,128)} %bitcast.101, f32[2,3072,256,4]{2,1,3,0:T(8,128)} %copy-done, f32[2,4,256]{2,1,0:T(4,128)S(1)} %fusion.2, f32[2,4,256]{2,1,0:T(4,128)S(1)} %get-tuple-element.33, pred[256,3072]{0,1:T(8,128)(4,1)} %add_add_fusion), kind=kOutput, calls=%fused_computation.26 | convolution fusion | flops 9689364480 | bytes 31219712 | tf_op jit(solution)/shard_map/hgts,shd->thgd/dot_general | solution.py:88
  482.0 33.5 %fusion = f32[2,4,256,3072]{2,3,1,0:T(8,128)} fusion(f32[2,4,256]{2,1,0:T(4,128)S(1)} %bitcast.115, f32[3072,2,128,1]{0,2,3,1:T(8,128)} %bitcast.102, f32[256,2,4,128]{0,3,2,1:T(8,128)S(1)} %bitcast.104, f32[2,4,256]{2,1,0:T(4,128)S(1)} %fusion.2, f32[2,4,256]{2,1,0:T(4,128)S(1)} %get-tuple-element.33, f32[2,3072,256,4]{2,1,3,0:T(8,128)} %copy-done, ...), kind=kOutput, calls=%fused_computation.1 | convolution fusion | flops 9701425152 | bytes 55336960 | tf_op jit(solution)/shard_map/thgd,shd->hgts/dot_general | solution.py:90
  515.6 29.4 %fusion.5 = f32[3072,2,128]{0,2,1:T(8,128)S(1)} fusion(f32[2,4,256,3072]{2,3,1,0:T(8,128)} %fusion, f32[256,2,4,128]{0,3,2,1:T(8,128)S(1)} %bitcast.99), kind=kOutput, calls=%fused_computation.10 | convolution fusion | flops 9664462848 | bytes 29360128 | tf_op jit(solution)/shard_map/hgts,thgd->shd/dot_general | solution.py:95
  545.0 7.7 broadcast.23.clone
  552.7 1.1 slice_dynamic-update-slice_fusion.1
  553.8 2.6 fusion.9
  556.4 2.4 fusion.8
  558.9 18.1 %convolution_multiply_fusion = f32[2,128,4,256]{3,1,2,0:T(8,128)} fusion(f32[3072,2,128,1]{0,2,3,1:T(8,128)S(1)} %bitcast.97, f32[2,4,256,3072]{2,3,1,0:T(8,128)} %fusion), kind=kOutput, calls=%fused_computation.14 | convolution fusion | flops 9663938560 | bytes 29360128 | tf_op jit(solution)/shard_map/hgts,shd->thgd/dot_general | solution.py:92
  576.9 2.5 copy.99
  579.5 2.5 copy.98
  582.0 225.7 %reduce-scatter.5.cloned.1.call-done = f32[256,256]{0,1:T(8,128)} async-done(((f32[16384,256]{0,1:T(8,128)}), f32[256,256]{0,1:T(8,128)}) %reduce-scatter.5.cloned.1.call-update) | async-done | bytes 262160 | tf_op jit(solution)/shard_map/reduce_scatter | solution.py:122
  808.8 50.3 %all_to_all.80 = f32[2,128,256]{2,1,0:T(8,128)S(1)} all-to-all(f32[2,128,256]{2,1,0:T(8,128)S(1)} %bitcast.109), channel_id=1, replica_groups=mesh['ctx'=64,'head'=2] {'head'}, dimensions={0} | all-to-all | bytes 524288 | tf_op jit(solution)/shard_map/all_to_all | solution.py:128
  860.1 332.5 %reduce-scatter.3.cloned.1.call-done = f32[256,256]{0,1:T(8,128)} async-done(((f32[16384,256]{0,1:T(8,128)}), f32[256,256]{0,1:T(8,128)}) %reduce-scatter.3.cloned.1.call-update) | async-done | bytes 262160 | tf_op jit(solution)/shard_map/reduce_scatter | solution.py:119
  1193.7 52.9 %all_to_all.81 = f32[2,128,256]{2,1,0:T(8,128)S(1)} all-to-all(f32[2,128,256]{2,1,0:T(8,128)S(1)} %bitcast.111), channel_id=1, replica_groups=mesh['ctx'=64,'head'=2] {'head'}, dimensions={0} | all-to-all | bytes 524288 | tf_op jit(solution)/shard_map/all_to_all | solution.py:127
  (48 shorter events, 10.2 us)
Async XLA Ops:
  7.2 355.8 %all-gather.2.cloned.1.call-start = ((), (), s32[]{:S(2)}) async-start(), calls=%async_computation.7 | async-start | bytes 17039360 | tf_op jit(solution)/shard_map/all_gather | solution.py:74
  27.4 11.8 copy-start.9
  27.4 15.7 %copy-start.5 = (f32[256,1024]{1,0:T(8,128)S(1)}, f32[256,1024]{1,0:T(8,128)}, u32[]{:S(2)}) copy-start(f32[256,1024]{1,0:T(8,128)} %param.5) | copy-start | bytes 3145732
  27.4 16.0 %copy-start.6 = (f32[256,1024]{1,0:T(8,128)S(1)}, f32[256,1024]{1,0:T(8,128)}, u32[]{:S(2)}) copy-start(f32[256,1024]{1,0:T(8,128)} %param.8) | copy-start | bytes 3145732
  27.4 302.0 %all-to-all-start.2 = ((f32[64,256,256]{1,2,0:T(8,128)}), f32[64,256,256]{1,2,0:T(8,128)}, u32[]{:S(2)}, u32[]{:S(2)}) async-start(f32[64,256,256]{1,2,0:T(8,128)} %stack.5), calls=%async_computation.2 | async-start | bytes 33554432 | tf_op jit(solution)/shard_map/all_to_all | solution.py:17
  39.1 768.7 %reduce-scatter.5.cloned.1.call-start = ((), (), s32[]{:S(2)}) async-start(), calls=%async_computation.9 | async-start | bytes 17039360 | tf_op jit(solution)/shard_map/reduce_scatter | solution.py:122
  362.9 5.2 copy-start.3
  368.1 22.8 %copy-start.1 = (f32[3072,256]{0,1:T(8,128)}, f32[3072,256]{0,1:T(8,128)S(1)}, u32[]{:S(2)}) copy-start(f32[3072,256]{0,1:T(8,128)S(1)} %pad_maximum_fusion.1) | copy-start | bytes 9437188
  390.9 8.7 copy-start
  390.9 14.1 %copy-start.7 = (f32[256,1024]{0,1:T(8,128)S(1)}, f32[256,1024]{0,1:T(8,128)}, u32[]{:S(2)}) copy-start(f32[256,1024]{0,1:T(8,128)} %copy.87) | copy-start | bytes 3145732
  453.5 739.1 %reduce-scatter.3.cloned.1.call-start = ((), (), s32[]{:S(2)}) async-start(), calls=%async_computation.8 | async-start | bytes 17039360 | tf_op jit(solution)/shard_map/reduce_scatter | solution.py:119
  456.7 25.3 %copy-start.4 = (pred[256,3072]{0,1:T(8,128)(4,1)S(1)}, pred[256,3072]{0,1:T(8,128)(4,1)}, u32[]{:S(2)}) copy-start(pred[256,3072]{0,1:T(8,128)(4,1)} %add_add_fusion) | copy-start | bytes 2359300
  456.7 25.3 %copy-start.8 = (f32[256,1024]{0,1:T(8,128)S(1)}, f32[256,1024]{0,1:T(8,128)}, u32[]{:S(2)}) copy-start(f32[256,1024]{0,1:T(8,128)} %copy.87) | copy-start | bytes 3145732
  552.7 6.2 copy-start.2
Sparse Core Ops, SparseCore 0:
  14.4 348.4 all-gather.1
  453.6 354.1 reduce-scatter.4
  810.2 382.4 reduce-scatter.2
